TPU v7x, 32 devices: a whole 2x2x4 slice. The times are simulated.
32 devices in a mesh: ep: 8 (over z, y), tp: 4 (over x, core).
Axes of the slice: x: 2, y: 2, z: 4, core: 2. Of those that a mesh axis runs over, the one named last changes fastest.
Arguments:
- tokens: bfloat16 [1024, 3584], P('ep', 'tp'), may hold values from -6 to 6
- tangents: bfloat16 [2, 1024, 3584], P(None, 'ep', 'tp'), may hold values from -6 to 6
- tangent_mask: int32 [2, 1024, 28], P(None, 'ep', 'tp'), may hold values 0 or 1
- expert_ids: int32 [1024, 2], P('ep'), may hold values from 0 to 7, all different within a row; in each aligned block of 128 rows (0 to 127, 128 to 255, ...) at most 48 rows name the same one
- gate_fixed: int32 [1024, 2], P('ep'), may hold values from 4096 to 65535
- w_up: bfloat16 [8, 3584, 1024], P('ep', None, 'tp'), may hold values from -0.09375 to 0.09375
- w_down: bfloat16 [8, 1024, 3584], P('ep', None, 'tp'), may hold values from -0.1875 to 0.1875
Outputs:
- mixed: bfloat16 [1024, 3584], P('ep', 'tp')
- mixed_tangents: bfloat16 [2, 1024, 3584], P(None, 'ep', 'tp')
Inputs may be any that keep to these rules, and one draw needn't show every extreme that they name: `expert_ids`: each row names 2 different experts; among the rows of the tokens of one index of ep (128 aligned rows) no expert is named by more than 48 rows, a bound that some block reaches.
All inputs are finite; a program needn't handle non-finite values. No bound on the sum of `tangent_mask` on one device may be relied on, other than what follows from the above.
Results may differ from a plain program's by a relative error of at most 0.008.
Values may be sent and summed in bfloat16 or wider, within the bound.
A program may use at most 64 MiB of HBM per device.

v0:
```python
import jax
import jax.numpy as jnp
from jax import lax
from jax.sharding import PartitionSpec as P


def body(tokens, tangents, tangent_mask, expert_ids, gate_fixed, w_up, w_down):
    group, quarter = tokens.shape
    n_ep = lax.axis_size("ep")
    top = expert_ids.shape[1]
    local_experts = w_up.shape[0]
    experts = local_experts * n_ep
    capacity = max(2, min(group, 3 * group * top // (2 * experts)))
    blocks = tangent_mask.shape[2]
    keep = tangent_mask.astype(jnp.bfloat16)
    masked = (tangents.reshape(2, group, blocks, quarter // blocks) * keep[..., None]).reshape(
        2, group, quarter
    )
    stacked = jnp.concatenate([tokens[None], masked], axis=0)
    flat_ids = expert_ids.reshape(-1)
    onehot = (flat_ids[:, None] == jnp.arange(experts, dtype=jnp.int32)[None, :]).astype(jnp.int32)
    rank = jnp.sum((jnp.cumsum(onehot, axis=0) - onehot) * onehot, axis=1)
    dest = flat_ids * capacity + rank
    owner = jnp.full((experts * capacity,), group, jnp.int32)
    owner = owner.at[dest].set(jnp.arange(group * top, dtype=jnp.int32) // top)
    send_cols = jnp.take(stacked, owner, axis=1, mode="fill", fill_value=0)
    send_cols = send_cols.reshape(3, n_ep, local_experts * capacity, quarter)
    arrived = lax.all_to_all(send_cols, "ep", split_axis=1, concat_axis=1, tiled=True)
    routed = arrived.reshape(3, n_ep, local_experts, capacity, quarter)
    weights = w_up
    hidden = jnp.einsum(
        "tsecd,edf->tsecf",
        lax.all_gather(routed, "tp", axis=4, tiled=True),
        weights,
        preferred_element_type=jnp.float32,
    )
    base = hidden[0]
    sig = jax.nn.sigmoid(base)
    slope = sig * (1.0 + base * (1.0 - sig))
    acts = jnp.concatenate([(base * sig)[None], slope[None] * hidden[1:]], axis=0).astype(
        jnp.bfloat16
    )
    out_width = w_down.shape[2]
    weights = w_down
    outs = jnp.einsum(
        "tsecf,efd->tsecd",
        lax.all_gather(acts, "tp", axis=4, tiled=True),
        weights,
        preferred_element_type=jnp.float32,
    ).astype(jnp.bfloat16)
    outs = outs.reshape(3, n_ep, local_experts * capacity, out_width)
    returned = lax.all_to_all(outs, "ep", split_axis=1, concat_axis=1, tiled=True)
    table = returned.reshape(3, experts * capacity, out_width)
    picked = jnp.take(table, dest, axis=1).reshape(3, group, top, out_width)
    gates = gate_fixed.astype(jnp.float32) / 65536.0
    summed = jnp.einsum("tgkd,gk->tgd", picked.astype(jnp.float32), gates).astype(jnp.bfloat16)
    return (summed[0], summed[1:])


def solution(mesh):
    placed = (
        P("ep", "tp"),
        P(None, "ep", "tp"),
        P(None, "ep", "tp"),
        P("ep", None),
        P("ep", None),
        P("ep", None, "tp"),
        P("ep", None, "tp"),
    )
    return jax.shard_map(
        body,
        mesh=mesh,
        in_specs=placed,
        out_specs=(P("ep", "tp"), P(None, "ep", "tp")),
        check_vma=False,
    )
```

profile of v0, /device:TPU:0, one launch (start us, length us, event | category | flops | bytes accessed | tf_op | source)
XLA Modules:
  0.0 249.6 jit_solution(13066110364712202970)
XLA Ops:
  7.2 0.0 copy-start
  7.2 0.0 copy-start.1
  7.2 0.0 all-gather.6.cloned.1.call-start
  7.2 1.0 copy.39
  8.2 0.1 eq.26
  8.3 0.1 reshape.144
  8.5 0.7 broadcast_multiply_fusion
  9.2 0.6 reduce-window.6
  9.8 0.2 slice_reduce_fusion
  10.0 0.1 copy.43
  10.1 0.1 mul.64
  10.3 0.1 fusion.16
  10.4 1.4 scatter_custom_fusion
  11.8 0.7 convert_element_type.38
  12.5 0.1 mul.65
  12.6 0.7 copy.46
  13.3 0.0 copy-done.1
  13.3 0.4 copy.47
  13.7 0.1 broadcast_in_dim.37
  13.8 1.6 copy_multiply_fusion
  15.4 0.9 pad_maximum_fusion
  16.4 5.0 %gather_fusion = bf16[384,3,896]{2,1,0:T(4,128)(2,1)} fusion(bf16[3,128,896]{2,0,1:T(4,128)(2,1)S(1)} %pad_maximum_fusion, s32[1024]{0:T(1024)S(1)} %pad_clamp_fusion.1), kind=kCustom, calls=%fused_computation | custom fusion | bytes 4130304 | tf_op jit(solution)/shard_map/jit(_take)/gather | solution.py:26
  21.4 2.2 copy_select_fusion
  23.6 54.6 %all_to_all.10 = bf16[3,8,48,896]{3,2,0,1:T(8,128)(2,1)S(1)} all-to-all(bf16[3,8,48,896]{3,2,0,1:T(8,128)(2,1)S(1)} %copy_select_fusion), channel_id=1, replica_groups=mesh['ep'=8,'tp'=4] {'ep'}, dimensions={1} | all-to-all | bytes 4128768 | tf_op jit(solution)/shard_map/all_to_all | solution.py:28
  78.2 1.6 copy.49
  79.8 0.0 all-gather.6.cloned.1.call-update
  79.8 0.0 all-gather.4.cloned.1.call-start
  79.9 56.6 %all-gather.6.cloned.1.call-done = bf16[3,8,48,3584]{3,2,1,0:T(8,128)(2,1)} async-done(((bf16[3,8,48,896]{3,2,1,0:T(8,128)(2,1)}), bf16[3,8,48,3584]{3,2,1,0:T(8,128)(2,1)}) %all-gather.6.cloned.1.call-update) | async-done | bytes 8257552 | tf_op jit(solution)/shard_map/all_gather | solution.py:33
  136.5 6.2 %fusion.8 = f32[3,8,1,48,256]{4,3,1,0,2:T(8,128)S(1)} fusion(bf16[3,8,48,3584]{3,2,1,0:T(8,128)(2,1)} %all-gather.6.cloned.1.call-done, bf16[1,3584,256]{2,1,0:T(8,128)(2,1)} %param.12), kind=kOutput, calls=%fused_computation.11 | convolution fusion | flops 2113929216 | bytes 11272192 | tf_op jit(solution)/shard_map/tsecd,edf->tsecf/dot_general | solution.py:31
  142.6 0.2 multiply_convert_fusion
  142.8 0.1 fusion.13
  142.9 0.9 pad_maximum_fusion.1
  143.8 0.0 all-gather.4.cloned.1.call-update
  143.8 24.5 %all-gather.4.cloned.1.call-done = bf16[3,8,1,48,1024]{4,3,1,0,2:T(8,128)(2,1)} async-done(((bf16[3,8,1,48,256]{4,3,1,0,2:T(8,128)(2,1)}), bf16[3,8,1,48,1024]{4,3,1,0,2:T(8,128)(2,1)}) %all-gather.4.cloned.1.call-update) | async-done | bytes 2359312 | tf_op jit(solution)/shard_map/all_gather | solution.py:47
  168.3 0.0 copy-done
  168.3 4.3 %fusion.2 = bf16[3,8,48,896]{3,2,1,0:T(8,128)(2,1)S(1)} fusion(bf16[3,8,1,48,1024]{4,3,1,0,2:T(8,128)(2,1)} %all-gather.4.cloned.1.call-done, bf16[1,1024,896]{2,1,0:T(8,128)(2,1)S(1)} %copy-done), kind=kOutput, calls=%fused_computation.6 | convolution fusion | flops 2114961408 | bytes 6258688 | tf_op jit(solution)/shard_map/tsecf,efd->tsecd/dot_general | solution.py:45
  172.6 1.5 copy.50
  174.1 0.0 copy-start.2
  174.1 0.0 copy-start.3
  174.1 5.6 %all-to-all-start.1 = ((bf16[3,8,48,896]{3,2,0,1:T(8,128)(2,1)}), bf16[3,8,48,896]{3,2,0,1:T(8,128)(2,1)}, u32[]{:S(2)}, u32[]{:S(2)}) async-start(bf16[3,8,48,896]{3,2,0,1:T(8,128)(2,1)} %copy.50), calls=%async_computation.1 | async-start | bytes 4128768 | tf_op jit(solution)/shard_map/all_to_all | solution.py:52
  179.7 0.1 reduce_sum.14
  179.9 0.1 copy.41
  179.9 0.0 copy-done.2
  180.0 0.1 copy.42
  180.1 0.0 copy-done.3
  180.1 0.1 copy.54
  180.3 47.5 %all-to-all-done.1 = bf16[3,8,48,896]{3,2,0,1:T(8,128)(2,1)} async-done(((bf16[3,8,48,896]{3,2,0,1:T(8,128)(2,1)}), bf16[3,8,48,896]{3,2,0,1:T(8,128)(2,1)}, u32[]{:S(2)}, u32[]{:S(2)}) %all-to-all-start.1) | async-done | bytes 2064416 | tf_op jit(solution)/shard_map/all_to_all | solution.py:52
  227.8 4.3 %copy.51 = bf16[3,8,48,896]{3,0,2,1:T(4,128)(2,1)} copy(bf16[3,8,48,896]{3,2,0,1:T(8,128)(2,1)} %all-to-all-done.1) | data formatting | bytes 4128768 | tf_op jit(solution)/shard_map/all_to_all | solution.py:52
  232.1 5.2 %gather_fusion.1 = bf16[256,3,896]{2,1,0:T(4,128)(2,1)} fusion(bf16[3,384,896]{2,0,1:T(4,128)(2,1)} %bitcast.63, s32[1024]{0:T(1024)S(1)} %pad_clamp_fusion), kind=kCustom, calls=%fused_computation.1 | custom fusion | bytes 2753536 | tf_op jit(solution)/shard_map/jit(_take)/gather | solution.py:54
  237.2 2.3 broadcast_select_fusion
  239.5 1.6 fusion.11
  241.1 0.1 copy.64
  241.2 0.8 slice.32
  242.0 0.7 slice_bitcast_fusion
  (12 shorter events, 0.1 us)
Async XLA Ops:
  7.2 161.1 %copy-start = (bf16[1,1024,896]{2,1,0:T(8,128)(2,1)S(1)}, bf16[1,1024,896]{2,1,0:T(8,128)(2,1)}, u32[]{:S(2)}) copy-start(bf16[1,1024,896]{2,1,0:T(8,128)(2,1)} %param.13) | copy-start | bytes 5505028
  7.2 6.2 %copy-start.1 = (bf16[128,896]{1,0:T(8,128)(2,1)S(1)}, bf16[128,896]{1,0:T(8,128)(2,1)}, u32[]{:S(2)}) copy-start(bf16[128,896]{1,0:T(8,128)(2,1)} %param.7) | copy-start | bytes 688132
  7.2 129.3 %all-gather.6.cloned.1.call-start = ((), (), s32[]{:S(2)}) async-start(), calls=%async_computation.3 | async-start | bytes 10321920 | tf_op jit(solution)/shard_map/all_gather | solution.py:33
  79.8 88.5 %all-gather.4.cloned.1.call-start = ((), (), s32[]{:S(2)}) async-start(), calls=%async_computation.2 | async-start | bytes 2949120 | tf_op jit(solution)/shard_map/all_gather | solution.py:47
  174.1 5.9 %copy-start.2 = (s32[128,2]{0,1:T(2,128)S(1)}, s32[128,2]{0,1:T(2,128)}, u32[]{:S(2)}) copy-start(s32[128,2]{0,1:T(2,128)} %param.10) | copy-start | bytes 3076
  174.1 6.0 %copy-start.3 = (s32[128,2]{0,1:T(2,128)S(1)}, s32[128,2]{0,1:T(2,128)}, u32[]{:S(2)}) copy-start(s32[128,2]{0,1:T(2,128)} %param.11) | copy-start | bytes 3076
  174.1 53.7 %all-to-all-start.1 = ((bf16[3,8,48,896]{3,2,0,1:T(8,128)(2,1)}), bf16[3,8,48,896]{3,2,0,1:T(8,128)(2,1)}, u32[]{:S(2)}, u32[]{:S(2)}) async-start(bf16[3,8,48,896]{3,2,0,1:T(8,128)(2,1)} %copy.50), calls=%async_computation.1 | async-start | bytes 4128768 | tf_op jit(solution)/shard_map/all_to_all | solution.py:52
Sparse Core Ops, SparseCore 0:
  79.9 56.4 all-gather.5
  143.9 24.3 all-gather.3
where the time goes:
time: 250 us
  waiting for transfers between devices  129 us (52%)
  blocking collectives  54.6 us (22%)
  local copies, waits for them, and re-layouts  24 us (10%)
  between operations  14.2 us (6%)
  matrix products  12.1 us (5%)
  other arithmetic  10.3 us (4%)
  starting transfers between devices  5.73 us (2%)
    all_gather x1, waiting for transfers between devices, body(): lax.all_gather(routed, 'tp', axis=4, tiled=True)  56.6 us
    all_to_all x1, blocking collectives, body(): lax.all_to_all(send_cols, 'ep', split_axis=1, concat_axis=1, tiled=True)  54.6 us
    all_to_all x1, waiting for transfers between devices, body(): lax.all_to_all(outs, 'ep', split_axis=1, concat_axis=1, tiled=True)  47.5 us
    all_gather x1, waiting for transfers between devices, body(): lax.all_gather(acts, 'tp', axis=4, tiled=True)  24.5 us
    dot_general x1, matrix products, body(): jnp.einsum('tsecd,edf->tsecf', lax.all_gather(routed, 'tp', axis=4, tiled...  6.16 us
    all_to_all x1, starting transfers between devices, body(): lax.all_to_all(outs, 'ep', split_axis=1, concat_axis=1, tiled=True)  5.65 us
    gather x1, local copies, waits for them, and re-layouts, body(): picked = jnp.take(table, dest, axis=1).reshape(3, group, top, out_width)  5.17 us
    gather x1, local copies, waits for them, and re-layouts, body(): send_cols = jnp.take(stacked, owner, axis=1, mode='fill', fill_value=0)  5.02 us
  transfers between devices with their start and end apart: 3, of which 3 were waited for; matrix products, arithmetic and copies ran while one was open for 0% of the time, Pallas kernels for 0%

commit v1 on v0

--- a/solution.py
+++ b/solution.py
@@ -1,7 +1,15 @@
+import functools
+
 import jax
 import jax.numpy as jnp
 from jax import lax
+from jax.experimental import pallas as pl
+from jax.experimental.pallas import tpu as pltpu
 from jax.sharding import PartitionSpec as P
+
+MESH = pl.DeviceIdType.MESH
+DISPATCH, ROW_X, ROW_CORE, ROW_DIAG, ACT_X, ACT_CORE, ACT_DIAG, RETURN = range(8)
+N_EP, N_TP = 8, 4
 
 
 def body(tokens, tangents, tangent_mask, expert_ids, gate_fixed, w_up, w_down):
@@ -57,6 +65,255 @@
     return (summed[0], summed[1:])
 
 
+def flip(e, position):
+    k = position // 2
+    dz = (k % 3 + 1) * ((k + 2) // 3)
+    bits = (position % 2, dz % 2, dz // 2)
+    own = (e % 2, (e // 2) % 2, e // 4)
+    mixed = [a + b - 2 * a * b for a, b in zip(own, bits)]
+    return mixed[0] + 2 * mixed[1] + 4 * mixed[2]
+
+
+def fused_kernel(
+    cap, tokens, tangents, mask, ids, gates, up_hbm, down_hbm, out, out_tangents,
+    stacked, pick, held, rows, acts, results, table, up, down, up_sem, down_sem, send, recv,
+):
+    e = lax.axis_index("ep")
+    p = lax.axis_index("tp")
+    group, quarter = tokens.shape
+    hidden = up.shape[1]
+    x, c = p // 2, p % 2
+    p_x = (1 - x) * 2 + c
+    p_core = x * 2 + (1 - c)
+
+    def copy(kind, i, src, dst, ep_to, tp_to):
+        return pltpu.make_async_remote_copy(
+            src_ref=src, dst_ref=dst, send_sem=send.at[kind, i], recv_sem=recv.at[kind, i],
+            device_id=(ep_to, tp_to), device_id_type=MESH,
+        )
+
+    def dispatch(i):
+        return copy(DISPATCH, i, held.at[i], rows.at[p, i], flip(e, i), p)
+
+    def row_x(i):
+        return copy(ROW_X, i, rows.at[p, i], rows.at[p, i], e, p_x)
+
+    def row_core(i):
+        return copy(ROW_CORE, i, rows.at[p, i], rows.at[p, i], e, p_core)
+
+    def row_diag(i):
+        return copy(ROW_DIAG, i, rows.at[p_x, i], rows.at[p_x, i], e, p_core)
+
+    def act_x(i):
+        return copy(ACT_X, i, acts.at[p, i], acts.at[p, i], e, p_x)
+
+    def act_core(i):
+        return copy(ACT_CORE, i, acts.at[p, i], acts.at[p, i], e, p_core)
+
+    def act_diag(i):
+        return copy(ACT_DIAG, i, acts.at[p_x, i], acts.at[p_x, i], e, p_core)
+
+    def give_back(i):
+        return copy(RETURN, i, results.at[i], table.at[i], flip(e, i), p)
+
+    load_up = pltpu.make_async_copy(up_hbm.at[0], up, up_sem)
+    load_down = pltpu.make_async_copy(down_hbm.at[0], down, down_sem)
+    load_up.start()
+    load_down.start()
+
+    barrier = pltpu.get_barrier_semaphore()
+    for i in range(1, N_EP):
+        pl.semaphore_signal(barrier, inc=1, device_id=(flip(e, i), p), device_id_type=MESH)
+    for peer in (p_x, p_core):
+        pl.semaphore_signal(barrier, inc=1, device_id=(e, peer), device_id_type=MESH)
+
+    stacked[0] = tokens[...]
+    blocks = mask.shape[2]
+    width = quarter // blocks
+    for d in range(2):
+        keep = mask[d].astype(jnp.float32)
+        for b in range(blocks):
+            part = tangents[d, :, b * width:(b + 1) * width].astype(jnp.float32)
+            stacked[1 + d, :, b * width:(b + 1) * width] = (part * keep[:, b:b + 1]).astype(jnp.bfloat16)
+
+    named = ids[...]
+    relative = jnp.bitwise_xor(named, e)
+    dz = relative // 2
+    position = jnp.where(dz == 0, 0, (dz + 1) % 3 + 1) * 2 + relative % 2
+    lane = lax.broadcasted_iota(jnp.int32, (group, group), 1)
+    line = lax.broadcasted_iota(jnp.int32, (group, group), 0)
+    first, second = position[:, 0:1] == lane, position[:, 1:2] == lane
+    member = jnp.where(first | second, 1.0, 0.0).astype(jnp.bfloat16)
+    before = jnp.where(lane < line, 1.0, 0.0).astype(jnp.bfloat16)
+    rank = jnp.dot(before, member, preferred_element_type=jnp.float32)
+    places = []
+    for k, match in enumerate((first, second)):
+        own_rank = jnp.sum(jnp.where(match, rank, 0.0), axis=1, keepdims=True).astype(jnp.int32)
+        places.append(position[:, k:k + 1] * cap + own_rank)
+    slot = lax.broadcasted_iota(jnp.int32, (group, N_EP * cap), 1)
+    hits = [place == slot for place in places]
+    chosen = jnp.where(hits[0] | hits[1], 1.0, 0.0)
+    pick[...] = jnp.transpose(chosen).astype(jnp.bfloat16).reshape(N_EP, cap, group)
+
+    pl.semaphore_wait(barrier, N_EP - 1 + 2)
+
+    def fill(i, target):
+        for t in range(3):
+            picked = jnp.dot(pick[i], stacked[t], preferred_element_type=jnp.float32)
+            target[t * cap:(t + 1) * cap, :] = picked.astype(jnp.bfloat16)
+
+    def send_one(i, carry):
+        fill(i, held.at[i])
+        dispatch(i).start()
+        return carry
+
+    fill(0, rows.at[p, 0])
+    lax.fori_loop(1, N_EP, send_one, 0)
+    load_up.wait()
+    load_down.wait()
+
+    def tick(n, carry):
+        @pl.when(n < N_EP)
+        def _():
+            @pl.when(n > 0)
+            def _():
+                dispatch(n).wait_recv()
+            row_x(n).start()
+            row_core(n).start()
+
+        @pl.when((n >= 1) & (n < N_EP + 1))
+        def _():
+            i = n - 1
+            row_x(i).wait_recv()
+            row_diag(i).start()
+            row_core(i).wait_recv()
+            row_diag(i).wait_recv()
+            total = jnp.zeros((3 * cap, hidden), jnp.float32)
+            for q in range(N_TP):
+                total += jnp.dot(
+                    rows[q, i], up[q * quarter:(q + 1) * quarter, :], preferred_element_type=jnp.float32
+                )
+            base = total[:cap]
+            sig = jax.nn.sigmoid(base)
+            slope = sig * (1.0 + base * (1.0 - sig))
+            acts[p, i, :cap, :] = (base * sig).astype(jnp.bfloat16)
+            acts[p, i, cap:2 * cap, :] = (slope * total[cap:2 * cap]).astype(jnp.bfloat16)
+            acts[p, i, 2 * cap:, :] = (slope * total[2 * cap:]).astype(jnp.bfloat16)
+            act_x(i).start()
+            act_core(i).start()
+
+        @pl.when(n >= 2)
+        def _():
+            i = n - 2
+            act_x(i).wait_recv()
+            act_diag(i).start()
+            act_core(i).wait_recv()
+            act_diag(i).wait_recv()
+            total = jnp.zeros((3 * cap, quarter), jnp.float32)
+            for q in range(N_TP):
+                total += jnp.dot(
+                    acts[q, i], down[q * hidden:(q + 1) * hidden, :], preferred_element_type=jnp.float32
+                )
+            rounded = total.astype(jnp.bfloat16)
+
+            @pl.when(i > 0)
+            def _():
+                results[i] = rounded
+                give_back(i).start()
+
+            @pl.when(i == 0)
+            def _():
+                table[0] = rounded
+
+        return carry
+
+    lax.fori_loop(0, N_EP + 2, tick, 0)
+
+    high, low = 0.0, 0.0
+    for k in range(2):
+        gate = gates[:, k:k + 1]
+        high += jnp.where(hits[k], (gate // 256).astype(jnp.float32), 0.0)
+        low += jnp.where(hits[k], (gate % 256).astype(jnp.float32), 0.0)
+    high, low = high.astype(jnp.bfloat16), low.astype(jnp.bfloat16)
+
+    def drain(i, carry):
+        for one in (row_x, row_core, row_diag, act_x, act_core, act_diag):
+            one(i).wait_send()
+
+        @pl.when(i > 0)
+        def _():
+            dispatch(i).wait_send()
+            give_back(i).wait_send()
+            give_back(i).wait_recv()
+
+        return carry
+
+    lax.fori_loop(0, N_EP, drain, 0)
+    for t in range(3):
+        back = table[:, t * cap:(t + 1) * cap, :].reshape(N_EP * cap, quarter)
+        total = 256.0 * jnp.dot(high, back, preferred_element_type=jnp.float32)
+        total += jnp.dot(low, back, preferred_element_type=jnp.float32)
+        total = (total * (1.0 / 65536.0)).astype(jnp.bfloat16)
+        if t == 0:
+            out[...] = total
+        else:
+            out_tangents[t - 1] = total
+
+
+def fused(tokens, tangents, tangent_mask, expert_ids, gate_fixed, w_up, w_down):
+    group, quarter = tokens.shape
+    cap = capacity_of(group, expert_ids.shape[1], N_EP)
+    depth, hidden = w_up.shape[1:]
+    vmem, hbm = pl.BlockSpec(memory_space=pltpu.VMEM), pl.BlockSpec(memory_space=pl.ANY)
+    bf16 = jnp.bfloat16
+    return pl.pallas_call(
+        functools.partial(fused_kernel, cap),
+        out_shape=(
+            jax.ShapeDtypeStruct((group, quarter), bf16),
+            jax.ShapeDtypeStruct((2, group, quarter), bf16),
+        ),
+        in_specs=[vmem] * 5 + [hbm] * 2,
+        out_specs=(vmem, vmem),
+        scratch_shapes=[
+            pltpu.VMEM((3, group, quarter), bf16),
+            pltpu.VMEM((N_EP, cap, group), bf16),
+            pltpu.VMEM((N_EP, 3 * cap, quarter), bf16),
+            pltpu.VMEM((N_TP, N_EP, 3 * cap, quarter), bf16),
+            pltpu.VMEM((N_TP, N_EP, 3 * cap, hidden), bf16),
+            pltpu.VMEM((N_EP, 3 * cap, quarter), bf16),
+            pltpu.VMEM((N_EP, 3 * cap, quarter), bf16),
+            pltpu.VMEM((depth, hidden), bf16),
+            pltpu.VMEM(w_down.shape[1:], bf16),
+            pltpu.SemaphoreType.DMA,
+            pltpu.SemaphoreType.DMA,
+            pltpu.SemaphoreType.DMA((8, N_EP)),
+            pltpu.SemaphoreType.DMA((8, N_EP)),
+        ],
+        compiler_params=pltpu.CompilerParams(
+            collective_id=0, has_side_effects=True, vmem_limit_bytes=56 * 1024 * 1024
+        ),
+    )(tokens, tangents, tangent_mask, expert_ids, gate_fixed, w_up, w_down)
+
+
+def capacity_of(group, top, experts):
+    return max(2, min(group, 3 * group * top // (2 * experts)))
+
+
+def any_body(*operands):
+    tokens, expert_ids, w_up = operands[0], operands[3], operands[5]
+    group, quarter = tokens.shape
+    fits = (
+        lax.axis_size("ep") == N_EP
+        and lax.axis_size("tp") == N_TP
+        and w_up.shape[0] == 1
+        and expert_ids.shape[1] == 2
+        and group == 128
+        and quarter % 128 == 0
+        and capacity_of(group, 2, N_EP) % 16 == 0
+    )
+    return (fused if fits else body)(*operands)
+
+
 def solution(mesh):
     placed = (
         P("ep", "tp"),
@@ -68,7 +325,7 @@
         P("ep", None, "tp"),
     )
     return jax.shard_map(
-        body,
+        any_body,
         mesh=mesh,
         in_specs=placed,
         out_specs=(P("ep", "tp"), P(None, "ep", "tp")),

time: 250 us -> 111 us (0.44)
  waiting for transfers between devices: 129 us -> 0 us
  Pallas kernels: 0 us -> 101 us
  blocking collectives: 54.6 us -> 0 us
  local copies, waits for them, and re-layouts: 24 us -> 7.77 us
  between operations: 14.2 us -> 0.64 us
  matrix products: 12.1 us -> 0 us
  other arithmetic: 10.3 us -> 0 us
  starting transfers between devices: 5.73 us -> 0 us
    pallas_call x0 -> x1, Pallas kernels: none -> 101 us  [fused(): pl.pallas_call(functools.partial(fused_kernel, cap), out_shape=(jax.Shape...]
    all_gather x2 -> x0, waiting for transfers between devices: 81.1 us -> none  [the longest x1 56.6 us: body(): lax.all_gather(routed, 'tp', axis=4, tiled=True)]
    all_to_all x1 -> x0, blocking collectives: 54.6 us -> none  [body(): lax.all_to_all(send_cols, 'ep', split_axis=1, concat_axis=1, tiled=True)]
    all_to_all x1 -> x0, waiting for transfers between devices: 47.5 us -> none  [body(): lax.all_to_all(outs, 'ep', split_axis=1, concat_axis=1, tiled=True)]
    dot_general x3 -> x0, matrix products: 12.1 us -> none  [the longest x1 6.16 us: body(): jnp.einsum('tsecd,edf->tsecf', lax.all_gather(routed, 'tp', axis=4, tiled...]
    gather x2 -> x0, local copies, waits for them, and re-layouts: 10.2 us -> none  [the longest x1 5.17 us: body(): picked = jnp.take(table, dest, axis=1).reshape(3, group, top, out_width)]
    unnamed x9 -> x5, local copies, waits for them, and re-layouts: 0.99 us -> 7.77 us
    all_to_all x2 -> x0, local copies, waits for them, and re-layouts: 5.84 us -> none  [the longest x1 4.29 us: body(): lax.all_to_all(outs, 'ep', split_axis=1, concat_axis=1, tiled=True)]
  transfers between devices with their start and end apart: 3 -> 0, of which waited for: 3 -> 0; matrix products, arithmetic and copies ran while one was open for 0% -> 0% of each run, Pallas kernels for 0% -> 0%
where the time goes in v1:
time: 111 us; the launch traced here: 109 us
  Pallas kernels  101 us (91%)
  local copies, waits for them, and re-layouts  7.77 us (7%)
    pallas_call x1, Pallas kernels, fused(): pl.pallas_call(functools.partial(fused_kernel, cap), out_shape=(jax.Shape...  101 us
    unnamed x5, local copies, waits for them, and re-layouts  7.77 us

profile of v1, /device:TPU:0, one launch (start us, length us, event | category | flops | bytes accessed | tf_op | source)
XLA Modules:
  0.0 109.4 jit_solution(2893418062740416793)
XLA Ops:
  0.6 1.4 %copy.10.ids = s32[128,2]{1,0:T(8,128)} copy(s32[128,2]{0,1:T(2,128)} %param.10) | data formatting | bytes 2048 | tf_op args[3]
  2.0 1.4 %copy.11.gates = s32[128,2]{1,0:T(8,128)} copy(s32[128,2]{0,1:T(2,128)} %param.11) | data formatting | bytes 2048 | tf_op args[4]
  3.5 1.5 %copy.9.mask = s32[2,128,7]{2,1,0:T(8,128)} copy(s32[2,128,7]{1,0,2:T(2,128)} %param.9) | data formatting | bytes 14336 | tf_op args[2]
  4.9 101.0 %shard_map.86 = (bf16[128,896]{1,0:T(8,128)(2,1)}, bf16[2,128,896]{2,1,0:T(8,128)(2,1)}) custom-call(bf16[128,896]{1,0:T(8,128)(2,1)} %tokens.1, bf16[2,128,896]{2,1,0:T(8,128)(2,1)} %tangents.1, s32[2,128,7]{2,1,0:T(8,128)} %copy.9.mask, s32[128,2]{1,0:T(8,128)} %copy.10.ids, s32[128,2]{1,0:T(8,128)} %copy.11.gates, bf16[1,3584,256]{2,1,0:T(8,128)(2,1)} %up_hbm.1, ...), custom_call_target="tpu_custom_call" | custom-call | tf_op jit(solution)/shard_map/pallas_call | solution.py:269
  105.9 1.6 %copy.14 = bf16[128,896]{1,0:T(8,128)(2,1)} copy(bf16[128,896]{1,0:T(8,128)(2,1)} %get-tuple-element.4) | data formatting | bytes 458752
  107.6 1.8 %copy.15 = bf16[2,128,896]{2,1,0:T(8,128)(2,1)} copy(bf16[2,128,896]{2,1,0:T(8,128)(2,1)} %get-tuple-element.5) | data formatting | bytes 917504

commit v2 on v0

--- a/solution.py
+++ b/solution.py
@@ -1,7 +1,15 @@
+import functools
+
 import jax
 import jax.numpy as jnp
 from jax import lax
+from jax.experimental import pallas as pl
+from jax.experimental.pallas import tpu as pltpu
 from jax.sharding import PartitionSpec as P
+
+MESH = pl.DeviceIdType.MESH
+ROW_X, ROW_CORE, ROW_DIAG, ACT_X, ACT_CORE, ACT_DIAG, NEAR, BACK, DENSE, RELAY, GATHER, PARTIAL = range(12)
+N_EP, N_TP = 8, 4
 
 
 def body(tokens, tangents, tangent_mask, expert_ids, gate_fixed, w_up, w_down):
@@ -57,6 +65,308 @@
     return (summed[0], summed[1:])
 
 
+HALF = N_EP // 2
+ORDER = (0, 1, 2, 4, 3, 5, 6)
+
+
+def flip(e, i):
+    bits = (e % 2, (e // 2) % 2, e // 4)
+    return sum((1 - bit if (i >> n) & 1 else bit) << n for n, bit in enumerate(bits))
+
+
+def fused_kernel(
+    cap, tokens, tangents, mask, ids, gates, up_hbm, down_hbm, out, out_tangents,
+    stacked, pick, weights, held, rows, acts, results, table,
+    dense, pick_in, weights_in, relayed, far_rows, far_acts, far_results, gathered, partial, partial_in, slopes,
+    up, down, up_sem, down_sem, send, recv,
+):
+    e = lax.axis_index("ep")
+    p = lax.axis_index("tp")
+    group, quarter = tokens.shape
+    hidden = up.shape[1]
+    x, c = p // 2, p % 2
+    p_x = (1 - x) * 2 + c
+    p_core = x * 2 + (1 - c)
+    started = []
+
+    def copy(kind, i, src, dst, ep_to, tp_to):
+        return pltpu.make_async_remote_copy(
+            src_ref=src, dst_ref=dst, send_sem=send.at[kind, i], recv_sem=recv.at[kind, i],
+            device_id=(ep_to, tp_to), device_id_type=MESH,
+        )
+
+    def start(one):
+        one.start()
+        started.append(one)
+
+    def spread(kind, u, q, peer):
+        buffers, at = (rows, far_rows) if kind <= ROW_DIAG else (acts, far_acts), u
+        ref = buffers[0].at[q, u] if u < HALF else buffers[1].at[q, at - HALF]
+        return copy(kind, u, ref, ref, e, peer)
+
+    def near(i):
+        return copy(NEAR, i, held.at[i], rows.at[p, i], flip(e, i), p)
+
+    def back(i):
+        return copy(BACK, i, results.at[i], table.at[i], flip(e, i), p)
+
+    def to_dense(t):
+        return copy(DENSE, t, stacked.at[t], dense.at[t], flip(e, HALF), p)
+
+    def to_pick():
+        return copy(DENSE, 3, pick.at[pl.ds(HALF, HALF)], pick_in, flip(e, HALF), p)
+
+    def to_weights():
+        return copy(DENSE, 4, weights.at[pl.ds(2, 2)], weights_in, flip(e, HALF), p)
+
+    def relay(t, r):
+        return copy(RELAY, t * HALF + r, relayed.at[t, r], far_rows.at[p, t, pl.ds(r * cap, cap)], flip(e, r), p)
+
+    def gather(t, r):
+        piece = pl.ds(r * cap, cap)
+        return copy(GATHER, t * HALF + r, far_results.at[t, piece], gathered.at[t, piece], flip(e, r), p)
+
+    def to_partial(t):
+        return copy(PARTIAL, t, partial.at[t], partial_in.at[t], flip(e, HALF), p)
+
+    load_up = pltpu.make_async_copy(up_hbm.at[0], up, up_sem)
+    load_down = pltpu.make_async_copy(down_hbm.at[0], down, down_sem)
+    load_up.start()
+    load_down.start()
+
+    barrier = pltpu.get_barrier_semaphore()
+    for i in range(1, HALF + 1):
+        pl.semaphore_signal(barrier, inc=1, device_id=(flip(e, i), p), device_id_type=MESH)
+    for peer in (p_x, p_core):
+        pl.semaphore_signal(barrier, inc=1, device_id=(e, peer), device_id_type=MESH)
+
+    stacked[0] = tokens[...]
+    blocks = mask.shape[2]
+    width = quarter // blocks
+    for d in range(2):
+        keep = mask[d].astype(jnp.float32)
+        for b in range(blocks):
+            part = tangents[d, :, b * width:(b + 1) * width].astype(jnp.float32)
+            stacked[1 + d, :, b * width:(b + 1) * width] = (part * keep[:, b:b + 1]).astype(jnp.bfloat16)
+
+    position = jnp.bitwise_xor(ids[...], e)
+    lane = lax.broadcasted_iota(jnp.int32, (group, group), 1)
+    line = lax.broadcasted_iota(jnp.int32, (group, group), 0)
+    first, second = position[:, 0:1] == lane, position[:, 1:2] == lane
+    member = jnp.where(first | second, 1.0, 0.0).astype(jnp.bfloat16)
+    before = jnp.where(lane < line, 1.0, 0.0).astype(jnp.bfloat16)
+    rank = jnp.dot(before, member, preferred_element_type=jnp.float32)
+    places = []
+    for k, match in enumerate((first, second)):
+        own_rank = jnp.sum(jnp.where(match, rank, 0.0), axis=1, keepdims=True).astype(jnp.int32)
+        places.append(position[:, k:k + 1] * cap + own_rank)
+    slot = lax.broadcasted_iota(jnp.int32, (group, N_EP * cap), 1)
+    chosen = jnp.where((places[0] == slot) | (places[1] == slot), 1.0, 0.0)
+    pick[...] = jnp.transpose(chosen).astype(jnp.bfloat16).reshape(N_EP, cap, group)
+
+    slot = lax.broadcasted_iota(jnp.int32, (group, HALF * cap), 1)
+    for half in range(2):
+        high, low = 0.0, 0.0
+        for k in range(2):
+            gate = gates[:, k:k + 1]
+            hit = places[k] == slot + half * HALF * cap
+            high += jnp.where(hit, (gate // 256).astype(jnp.float32), 0.0)
+            low += jnp.where(hit, (gate % 256).astype(jnp.float32), 0.0)
+        weights[2 * half] = high.astype(jnp.bfloat16)
+        weights[2 * half + 1] = low.astype(jnp.bfloat16)
+
+    pl.semaphore_wait(barrier, HALF + 2)
+    start(to_pick())
+    start(to_dense(0))
+
+    def select(one_hot, source):
+        return jnp.dot(one_hot, source, preferred_element_type=jnp.float32).astype(jnp.bfloat16)
+
+    def combine(high, low, outs):
+        total = 256.0 * jnp.dot(high, outs, preferred_element_type=jnp.float32)
+        total += jnp.dot(low, outs, preferred_element_type=jnp.float32)
+        return total * (1.0 / 65536.0)
+
+    for t in range(3):
+        rows[p, 0, t * cap:(t + 1) * cap, :] = select(pick[0], stacked[t])
+    for i in range(1, HALF):
+        for t in range(3):
+            held[i, t * cap:(t + 1) * cap, :] = select(pick[i], stacked[t])
+        start(near(i))
+    start(to_dense(1))
+    start(to_dense(2))
+    start(to_weights())
+    load_up.wait()
+    load_down.wait()
+
+    def pass_on(t):
+        if t == 0:
+            to_pick().wait_recv()
+        to_dense(t).wait_recv()
+        for r in range(1, HALF):
+            relayed[t, r] = select(pick_in[r], dense[t])
+            start(relay(t, r))
+        far_rows[p, t, :cap, :] = select(pick_in[0], dense[t])
+
+    def arrive(u):
+        if 0 < u < HALF:
+            near(u).wait_recv()
+        if u >= HALF:
+            for r in range(1, HALF):
+                relay(u - HALF, r).wait_recv()
+        start(spread(ROW_X, u, p, p_x))
+        start(spread(ROW_CORE, u, p, p_core))
+
+    def product(buffers, u, matrix, depth):
+        total = 0.0
+        for q in range(N_TP):
+            left = buffers[0][q, u] if u < HALF else buffers[1][q, u - HALF]
+            total += jnp.dot(left, matrix[q * depth:(q + 1) * depth, :], preferred_element_type=jnp.float32)
+        return total
+
+    def go_up(u):
+        spread(ROW_X, u, p, p_x).wait_recv()
+        start(spread(ROW_DIAG, u, p_x, p_core))
+        spread(ROW_CORE, u, p, p_core).wait_recv()
+        spread(ROW_DIAG, u, p_x, p_core).wait_recv()
+        total = product((rows, far_rows), u, up, quarter)
+        if u < HALF or u == HALF:
+            base = total[:cap] if u < HALF else total
+            sig = jax.nn.sigmoid(base)
+            slope = sig * (1.0 + base * (1.0 - sig))
+            act = (base * sig).astype(jnp.bfloat16)
+        if u < HALF:
+            acts[p, u, :cap, :] = act
+            acts[p, u, cap:2 * cap, :] = (slope * total[cap:2 * cap]).astype(jnp.bfloat16)
+            acts[p, u, 2 * cap:, :] = (slope * total[2 * cap:]).astype(jnp.bfloat16)
+        elif u == HALF:
+            slopes[...] = slope
+            far_acts[p, 0] = act
+        else:
+            far_acts[p, u - HALF] = (slopes[...] * total).astype(jnp.bfloat16)
+        start(spread(ACT_X, u, p, p_x))
+        start(spread(ACT_CORE, u, p, p_core))
+
+    def go_down(u):
+        spread(ACT_X, u, p, p_x).wait_recv()
+        start(spread(ACT_DIAG, u, p_x, p_core))
+        spread(ACT_CORE, u, p, p_core).wait_recv()
+        spread(ACT_DIAG, u, p_x, p_core).wait_recv()
+        rounded = product((acts, far_acts), u, down, hidden).astype(jnp.bfloat16)
+        if u == 0:
+            table[0] = rounded
+        elif u < HALF:
+            results[u] = rounded
+            start(back(u))
+        else:
+            t = u - HALF
+            gathered[t, :cap, :] = rounded[:cap]
+            far_results[t, cap:, :] = rounded[cap:]
+            for r in range(1, HALF):
+                start(gather(t, r))
+
+    def hand_over(t):
+        if t == 0:
+            to_weights().wait_recv()
+        for r in range(1, HALF):
+            gather(t, r).wait_recv()
+        partial[t] = combine(weights_in[0], weights_in[1], gathered[t]).astype(jnp.bfloat16)
+        start(to_partial(t))
+
+    last = len(ORDER)
+    for n in range(last + 3):
+        if n in (2, 4, 6):
+            pass_on(n // 2 - 1)
+        if n < last:
+            arrive(ORDER[n])
+        if 1 <= n < last + 1:
+            go_up(ORDER[n - 1])
+        if 2 <= n < last + 2:
+            go_down(ORDER[n - 2])
+        if n >= 3 and ORDER[n - 3] >= HALF:
+            hand_over(ORDER[n - 3] - HALF)
+
+    for i in range(1, HALF):
+        back(i).wait_recv()
+    for t in range(3):
+        outs = table[:, t * cap:(t + 1) * cap, :].reshape(HALF * cap, quarter)
+        total = combine(weights[0], weights[1], outs)
+        to_partial(t).wait_recv()
+        total = (total + partial_in[t].astype(jnp.float32)).astype(jnp.bfloat16)
+        if t == 0:
+            out[...] = total
+        else:
+            out_tangents[t - 1] = total
+    for one in started:
+        one.wait_send()
+
+
+def fused(tokens, tangents, tangent_mask, expert_ids, gate_fixed, w_up, w_down):
+    group, quarter = tokens.shape
+    cap = capacity_of(group, expert_ids.shape[1], N_EP)
+    depth, hidden = w_up.shape[1:]
+    vmem, hbm = pl.BlockSpec(memory_space=pltpu.VMEM), pl.BlockSpec(memory_space=pl.ANY)
+    bf16 = jnp.bfloat16
+    return pl.pallas_call(
+        functools.partial(fused_kernel, cap),
+        out_shape=(
+            jax.ShapeDtypeStruct((group, quarter), bf16),
+            jax.ShapeDtypeStruct((2, group, quarter), bf16),
+        ),
+        in_specs=[vmem] * 5 + [hbm] * 2,
+        out_specs=(vmem, vmem),
+        scratch_shapes=[
+            pltpu.VMEM((3, group, quarter), bf16),
+            pltpu.VMEM((N_EP, cap, group), bf16),
+            pltpu.VMEM((4, group, HALF * cap), bf16),
+            pltpu.VMEM((HALF, 3 * cap, quarter), bf16),
+            pltpu.VMEM((N_TP, HALF, 3 * cap, quarter), bf16),
+            pltpu.VMEM((N_TP, HALF, 3 * cap, hidden), bf16),
+            pltpu.VMEM((HALF, 3 * cap, quarter), bf16),
+            pltpu.VMEM((HALF, 3 * cap, quarter), bf16),
+            pltpu.VMEM((3, group, quarter), bf16),
+            pltpu.VMEM((HALF, cap, group), bf16),
+            pltpu.VMEM((2, group, HALF * cap), bf16),
+            pltpu.VMEM((3, HALF, cap, quarter), bf16),
+            pltpu.VMEM((N_TP, 3, HALF * cap, quarter), bf16),
+            pltpu.VMEM((N_TP, 3, HALF * cap, hidden), bf16),
+            pltpu.VMEM((3, HALF * cap, quarter), bf16),
+            pltpu.VMEM((3, HALF * cap, quarter), bf16),
+            pltpu.VMEM((3, group, quarter), bf16),
+            pltpu.VMEM((3, group, quarter), bf16),
+            pltpu.VMEM((HALF * cap, hidden), jnp.float32),
+            pltpu.VMEM((depth, hidden), bf16),
+            pltpu.VMEM(w_down.shape[1:], bf16),
+            pltpu.SemaphoreType.DMA,
+            pltpu.SemaphoreType.DMA,
+            pltpu.SemaphoreType.DMA((12, 3 * HALF)),
+            pltpu.SemaphoreType.DMA((12, 3 * HALF)),
+        ],
+        compiler_params=pltpu.CompilerParams(
+            collective_id=0, has_side_effects=True, vmem_limit_bytes=56 * 1024 * 1024
+        ),
+    )(tokens, tangents, tangent_mask, expert_ids, gate_fixed, w_up, w_down)
+
+
+def capacity_of(group, top, experts):
+    return max(2, min(group, 3 * group * top // (2 * experts)))
+
+
+def any_body(*operands):
+    tokens, expert_ids, w_up = operands[0], operands[3], operands[5]
+    group, quarter = tokens.shape
+    fits = (
+        lax.axis_size("ep") == N_EP
+        and lax.axis_size("tp") == N_TP
+        and w_up.shape[0] == 1
+        and expert_ids.shape[1] == 2
+        and group == 128
+        and quarter % 128 == 0
+        and capacity_of(group, 2, N_EP) % 16 == 0
+    )
+    return (fused if fits else body)(*operands)
+
+
 def solution(mesh):
     placed = (
         P("ep", "tp"),
@@ -68,7 +378,7 @@
         P("ep", None, "tp"),
     )
     return jax.shard_map(
-        body,
+        any_body,
         mesh=mesh,
         in_specs=placed,
         out_specs=(P("ep", "tp"), P(None, "ep", "tp")),

time: 250 us -> 126 us (0.50)
  waiting for transfers between devices: 129 us -> 0 us
  Pallas kernels: 0 us -> 118 us
  blocking collectives: 54.6 us -> 0 us
  local copies, waits for them, and re-layouts: 24 us -> 7.77 us
  between operations: 14.2 us -> 0.64 us
  matrix products: 12.1 us -> 0 us
  other arithmetic: 10.3 us -> 0 us
  starting transfers between devices: 5.73 us -> 0 us
    pallas_call x0 -> x1, Pallas kernels: none -> 118 us  [fused(): pl.pallas_call(functools.partial(fused_kernel, cap), out_shape=(jax.Shape...]
    all_gather x2 -> x0, waiting for transfers between devices: 81.1 us -> none  [the longest x1 56.6 us: body(): lax.all_gather(routed, 'tp', axis=4, tiled=True)]
    all_to_all x1 -> x0, blocking collectives: 54.6 us -> none  [body(): lax.all_to_all(send_cols, 'ep', split_axis=1, concat_axis=1, tiled=True)]
    all_to_all x1 -> x0, waiting for transfers between devices: 47.5 us -> none  [body(): lax.all_to_all(outs, 'ep', split_axis=1, concat_axis=1, tiled=True)]
    dot_general x3 -> x0, matrix products: 12.1 us -> none  [the longest x1 6.16 us: body(): jnp.einsum('tsecd,edf->tsecf', lax.all_gather(routed, 'tp', axis=4, tiled...]
    gather x2 -> x0, local copies, waits for them, and re-layouts: 10.2 us -> none  [the longest x1 5.17 us: body(): picked = jnp.take(table, dest, axis=1).reshape(3, group, top, out_width)]
    unnamed x9 -> x5, local copies, waits for them, and re-layouts: 0.99 us -> 7.77 us
    all_to_all x2 -> x0, local copies, waits for them, and re-layouts: 5.84 us -> none  [the longest x1 4.29 us: body(): lax.all_to_all(outs, 'ep', split_axis=1, concat_axis=1, tiled=True)]
  transfers between devices with their start and end apart: 3 -> 0, of which waited for: 3 -> 0; matrix products, arithmetic and copies ran while one was open for 0% -> 0% of each run, Pallas kernels for 0% -> 0%
where the time goes in v2:
time: 126 us
  Pallas kernels  118 us (94%)
  local copies, waits for them, and re-layouts  7.77 us (6%)
    pallas_call x1, Pallas kernels, fused(): pl.pallas_call(functools.partial(fused_kernel, cap), out_shape=(jax.Shape...  118 us
    unnamed x5, local copies, waits for them, and re-layouts  7.77 us

profile of v2, /device:TPU:0, one launch (start us, length us, event | category | flops | bytes accessed | tf_op | source)
XLA Modules:
  0.0 126.1 jit_solution(17524109811361263444)
XLA Ops:
  0.6 1.4 %copy.10.ids = s32[128,2]{1,0:T(8,128)} copy(s32[128,2]{0,1:T(2,128)} %param.10) | data formatting | bytes 2048 | tf_op args[3]
  2.0 1.4 %copy.11.gates = s32[128,2]{1,0:T(8,128)} copy(s32[128,2]{0,1:T(2,128)} %param.11) | data formatting | bytes 2048 | tf_op args[4]
  3.5 1.5 %copy.9.mask = s32[2,128,7]{2,1,0:T(8,128)} copy(s32[2,128,7]{1,0,2:T(2,128)} %param.9) | data formatting | bytes 14336 | tf_op args[2]
  4.9 117.7 %shard_map.86 = (bf16[128,896]{1,0:T(8,128)(2,1)}, bf16[2,128,896]{2,1,0:T(8,128)(2,1)}) custom-call(bf16[128,896]{1,0:T(8,128)(2,1)} %tokens.1, bf16[2,128,896]{2,1,0:T(8,128)(2,1)} %tangents.1, s32[2,128,7]{2,1,0:T(8,128)} %copy.9.mask, s32[128,2]{1,0:T(8,128)} %copy.10.ids, s32[128,2]{1,0:T(8,128)} %copy.11.gates, bf16[1,3584,256]{2,1,0:T(8,128)(2,1)} %up_hbm.1, ...), custom_call_target="tpu_custom_call" | custom-call | tf_op jit(solution)/shard_map/pallas_call | solution.py:310
  122.7 1.6 %copy.14 = bf16[128,896]{1,0:T(8,128)(2,1)} copy(bf16[128,896]{1,0:T(8,128)(2,1)} %get-tuple-element.4) | data formatting | bytes 458752
  124.3 1.8 %copy.15 = bf16[2,128,896]{2,1,0:T(8,128)(2,1)} copy(bf16[2,128,896]{2,1,0:T(8,128)(2,1)} %get-tuple-element.5) | data formatting | bytes 917504

commit v3 on v1

--- a/solution.py
+++ b/solution.py
@@ -67,7 +67,7 @@
 
 def flip(e, position):
     k = position // 2
-    dz = (k % 3 + 1) * ((k + 2) // 3)
+    dz = k
     bits = (position % 2, dz % 2, dz // 2)
     own = (e % 2, (e // 2) % 2, e // 4)
     mixed = [a + b - 2 * a * b for a, b in zip(own, bits)]
@@ -76,7 +76,7 @@
 
 def fused_kernel(
     cap, tokens, tangents, mask, ids, gates, up_hbm, down_hbm, out, out_tangents,
-    stacked, pick, held, rows, acts, results, table, up, down, up_sem, down_sem, send, recv,
+    stacked, pick, held, rows, acts, results, table, early, lines, up, down, up_sem, down_sem, send, recv,
 ):
     e = lax.axis_index("ep")
     p = lax.axis_index("tp")
@@ -127,19 +127,24 @@
     for peer in (p_x, p_core):
         pl.semaphore_signal(barrier, inc=1, device_id=(e, peer), device_id_type=MESH)
 
+    lines[...] = jnp.zeros_like(lines)
+    lines[0:2, :] = ids[...]
+    lines[2:4, :] = gates[...]
+    for b in range(mask.shape[0]):
+        lines[4 + 2 * b:6 + 2 * b, :] = mask[b]
+    by_token = jnp.transpose(lines[...].astype(jnp.float32))
+    small = by_token.astype(jnp.int32)
+
     stacked[0] = tokens[...]
-    blocks = mask.shape[2]
+    blocks = mask.shape[0]
     width = quarter // blocks
     for d in range(2):
-        keep = mask[d].astype(jnp.float32)
+        keep = by_token[:, 4:4 + 2 * blocks]
         for b in range(blocks):
             part = tangents[d, :, b * width:(b + 1) * width].astype(jnp.float32)
-            stacked[1 + d, :, b * width:(b + 1) * width] = (part * keep[:, b:b + 1]).astype(jnp.bfloat16)
-
-    named = ids[...]
-    relative = jnp.bitwise_xor(named, e)
-    dz = relative // 2
-    position = jnp.where(dz == 0, 0, (dz + 1) % 3 + 1) * 2 + relative % 2
+            stacked[1 + d, :, b * width:(b + 1) * width] = (part * keep[:, 2 * b + d:2 * b + d + 1]).astype(jnp.bfloat16)
+
+    position = jnp.bitwise_xor(small[:, 0:2], e)
     lane = lax.broadcasted_iota(jnp.int32, (group, group), 1)
     line = lax.broadcasted_iota(jnp.int32, (group, group), 0)
     first, second = position[:, 0:1] == lane, position[:, 1:2] == lane
@@ -229,12 +234,21 @@
 
     lax.fori_loop(0, N_EP + 2, tick, 0)
 
-    high, low = 0.0, 0.0
-    for k in range(2):
-        gate = gates[:, k:k + 1]
-        high += jnp.where(hits[k], (gate // 256).astype(jnp.float32), 0.0)
-        low += jnp.where(hits[k], (gate % 256).astype(jnp.float32), 0.0)
-    high, low = high.astype(jnp.bfloat16), low.astype(jnp.bfloat16)
+    def combine(t, lo_at, hi_at):
+        columns = lax.broadcasted_iota(jnp.int32, (group, (hi_at - lo_at) * cap), 1) + lo_at * cap
+        high, low = 0.0, 0.0
+        for k in range(2):
+            gate = small[:, 2 + k:3 + k]
+            hit = places[k] == columns
+            high += jnp.where(hit, (gate // 256).astype(jnp.float32), 0.0)
+            low += jnp.where(hit, (gate % 256).astype(jnp.float32), 0.0)
+        back = table[lo_at:hi_at, t * cap:(t + 1) * cap, :].reshape((hi_at - lo_at) * cap, quarter)
+        total = 256.0 * jnp.dot(high.astype(jnp.bfloat16), back, preferred_element_type=jnp.float32)
+        return total + jnp.dot(low.astype(jnp.bfloat16), back, preferred_element_type=jnp.float32)
+
+    def returned(i, carry):
+        give_back(i).wait_recv()
+        return carry
 
     def drain(i, carry):
         for one in (row_x, row_core, row_diag, act_x, act_core, act_diag):
@@ -243,21 +257,27 @@
         @pl.when(i > 0)
         def _():
             dispatch(i).wait_send()
-            give_back(i).wait_send()
-            give_back(i).wait_recv()
-
-        return carry
-
+
+        return carry
+
+    lax.fori_loop(1, N_EP - 2, returned, 0)
+    for t in range(3):
+        early[t] = combine(t, 0, N_EP - 2)
     lax.fori_loop(0, N_EP, drain, 0)
+    lax.fori_loop(N_EP - 2, N_EP, returned, 0)
     for t in range(3):
-        back = table[:, t * cap:(t + 1) * cap, :].reshape(N_EP * cap, quarter)
-        total = 256.0 * jnp.dot(high, back, preferred_element_type=jnp.float32)
-        total += jnp.dot(low, back, preferred_element_type=jnp.float32)
+        total = early[t] + combine(t, N_EP - 2, N_EP)
         total = (total * (1.0 / 65536.0)).astype(jnp.bfloat16)
         if t == 0:
             out[...] = total
         else:
             out_tangents[t - 1] = total
+
+    def sent(i, carry):
+        give_back(i).wait_send()
+        return carry
+
+    lax.fori_loop(1, N_EP, sent, 0)
 
 
 def fused(tokens, tangents, tangent_mask, expert_ids, gate_fixed, w_up, w_down):
@@ -282,6 +302,8 @@
             pltpu.VMEM((N_TP, N_EP, 3 * cap, hidden), bf16),
             pltpu.VMEM((N_EP, 3 * cap, quarter), bf16),
             pltpu.VMEM((N_EP, 3 * cap, quarter), bf16),
+            pltpu.VMEM((3, group, quarter), jnp.float32),
+            pltpu.VMEM((group, group), jnp.int32),
             pltpu.VMEM((depth, hidden), bf16),
             pltpu.VMEM(w_down.shape[1:], bf16),
             pltpu.SemaphoreType.DMA,
@@ -292,7 +314,7 @@
         compiler_params=pltpu.CompilerParams(
             collective_id=0, has_side_effects=True, vmem_limit_bytes=56 * 1024 * 1024
         ),
-    )(tokens, tangents, tangent_mask, expert_ids, gate_fixed, w_up, w_down)
+    )(tokens, tangents, tangent_mask.transpose(2, 0, 1), expert_ids.T, gate_fixed.T, w_up, w_down)
 
 
 def capacity_of(group, top, experts):
@@ -309,6 +331,7 @@
         and expert_ids.shape[1] == 2
         and group == 128
         and quarter % 128 == 0
+        and 4 + 2 * operands[2].shape[2] <= group
         and capacity_of(group, 2, N_EP) % 16 == 0
     )
     return (fused if fits else body)(*operands)

time: 111 us -> 105 us (0.946)
  the two profiles are of different devices: /device:TPU:0 before, /device:TPU:8 now
where the time goes in v3:
time: 105 us
  Pallas kernels  101 us (96%)
  local copies, waits for them, and re-layouts  3.47 us (3%)
    pallas_call x1, Pallas kernels, fused(): pl.pallas_call(functools.partial(fused_kernel, cap), out_shape=(jax.Shape...  101 us
    unnamed x2, local copies, waits for them, and re-layouts  3.47 us

profile of v3, /device:TPU:8, one launch (start us, length us, event | category | flops | bytes accessed | tf_op | source)
XLA Modules:
  0.0 105.2 jit_solution(980302324535810649)
XLA Ops:
  0.6 101.1 %shard_map.86 = (bf16[128,896]{1,0:T(8,128)(2,1)}, bf16[2,128,896]{2,1,0:T(8,128)(2,1)}) custom-call(bf16[128,896]{1,0:T(8,128)(2,1)} %tokens.1, bf16[2,128,896]{2,1,0:T(8,128)(2,1)} %tangents.1, s32[7,2,128]{2,1,0:T(2,128)} %bitcast.3, s32[2,128]{1,0:T(2,128)} %bitcast.4, s32[2,128]{1,0:T(2,128)} %bitcast.5, bf16[1,3584,256]{2,1,0:T(8,128)(2,1)} %up_hbm.1, ...), custom_call_target="tpu_custom_call" | custom-call | tf_op jit(solution)/shard_map/pallas_call | solution.py:289
  101.7 1.6 %copy.11 = bf16[128,896]{1,0:T(8,128)(2,1)} copy(bf16[128,896]{1,0:T(8,128)(2,1)} %get-tuple-element.4) | data formatting | bytes 458752
  103.4 1.8 %copy.12 = bf16[2,128,896]{2,1,0:T(8,128)(2,1)} copy(bf16[2,128,896]{2,1,0:T(8,128)(2,1)} %get-tuple-element.5) | data formatting | bytes 917504
